TPU v7x, 32 devices: a whole 2x2x4 slice. The times are simulated.
32 devices in a mesh: rows: 8 (over y, x, core), cols: 4 (over z).
Axes of the slice: x: 2, y: 2, z: 4, core: 2. Of those that a mesh axis runs over, the one named last changes fastest.
Arguments:
- grads: bfloat16 [9216, 8192], P(('rows', 'cols')), may hold values from -6 to 6
- tests: float32 [64, 8192], P(None, 'cols'), may hold values from -6 to 6
Outputs:
- solution: float32 [64, 8192], P(None, 'cols')
- scores: float32 [64, 9216], P(None, ('rows', 'cols'))
All inputs are finite; a program needn't handle non-finite values.
Results may differ from a plain program's by a relative error of at most 0.0041.
Values may be sent and summed in bfloat16 or wider, within the bound.
A program may use at most 64 MiB of HBM per device.

v0:
```python
import jax
import jax.numpy as jnp
from jax import lax
from jax.sharding import PartitionSpec as P

ITERS = 2
damping = 0.5


def per_device(grads, tests):
    n_rows = lax.axis_size("rows")
    n_cols = lax.axis_size("cols")
    n_total = grads.shape[0] * n_rows * n_cols
    width = grads.shape[1]
    solution = jnp.zeros(tests.shape, jnp.float32)
    residual = tests
    direction = tests
    norm_now = lax.psum(jnp.sum(residual * residual, axis=1), "cols")
    for step in range(ITERS):
        proj = lax.dot_general(
            grads,
            lax.all_gather(direction.astype(jnp.bfloat16), "cols", axis=1, tiled=True),
            (((1,), (1,)), ((), ())),
            preferred_element_type=jnp.float32,
        ).astype(jnp.bfloat16)
        partial_value = lax.dot_general(
            proj, grads, (((0,), (0,)), ((), ())), preferred_element_type=jnp.float32
        )
        owned = lax.psum_scatter(partial_value, "cols", scatter_dimension=1, tiled=True)
        owned = lax.psum(owned, "rows")
        image = owned / n_total + damping * direction
        curv, cross, image_sq = lax.psum(
            (
                jnp.sum(direction * image, axis=1),
                jnp.sum(residual * image, axis=1),
                jnp.sum(image * image, axis=1),
            ),
            "cols",
        )
        alpha = norm_now / curv
        norm_next = norm_now - 2.0 * alpha * cross + alpha * alpha * image_sq
        solution = solution + alpha[:, None] * direction
        residual = residual - alpha[:, None] * image
        if step + 1 < ITERS:
            direction = residual + (norm_next / norm_now)[:, None] * direction
            norm_now = norm_next
    scores = lax.dot_general(
        lax.all_gather(solution.astype(jnp.bfloat16), "cols", axis=1, tiled=True),
        grads,
        (((1,), (1,)), ((), ())),
        preferred_element_type=jnp.float32,
    )
    return (solution, scores * width ** (-0.5))


def solution(mesh):
    placed = (P(("rows", "cols"), None), P(None, "cols"))
    return jax.shard_map(
        per_device,
        mesh=mesh,
        in_specs=placed,
        out_specs=(P(None, "cols"), P(None, ("rows", "cols"))),
        check_vma=False,
    )
```

profile of v0, /device:TPU:0, one launch (start us, length us, event | category | flops | bytes accessed | tf_op | source)
XLA Modules:
  0.0 350.8 jit_solution(4595125535650454993)
XLA Ops:
  7.2 0.0 all-gather.4.cloned.1.call-start
  7.2 1.8 convert_element_type.16
  9.0 0.0 reduce-scatter.3.cloned.1.call-start
  9.1 31.8 %all-gather.4.cloned.1.call-done = bf16[64,8192]{1,0:T(8,128)(2,1)} async-done(((bf16[64,2048]{1,0:T(8,128)(2,1)}), bf16[64,8192]{1,0:T(8,128)(2,1)}) %all-gather.4.cloned.1.call-update) | async-done | bytes 1048592 | tf_op jit(solution)/shard_map/all_gather | solution.py:22
  40.9 9.4 %fusion = f32[64,8192]{1,0:T(8,128)} fusion(bf16[288,8192]{1,0:T(8,128)(2,1)} %param.2, bf16[64,8192]{1,0:T(8,128)(2,1)} %all-gather.4.cloned.1.call-done), kind=kOutput, calls=%fused_computation.2 | convolution fusion | flops 603998208 | bytes 7864320 | tf_op jit(solution)/shard_map/dot_general | solution.py:26
  50.3 0.0 all-reduce.4.cloned.1.call-start
  50.4 43.1 %reduce-scatter.3.cloned.1.call-done = f32[64,2048]{1,0:T(8,128)} async-done(((f32[64,8192]{1,0:T(8,128)}), f32[64,2048]{1,0:T(8,128)}) %reduce-scatter.3.cloned.1.call-update) | async-done | bytes 524304 | tf_op jit(solution)/shard_map/reduce_scatter | solution.py:29
  93.5 0.0 all-gather.6.cloned.1.call-start
  93.5 57.1 %all-reduce.4.cloned.1.call-done = f32[64,2048]{1,0:T(8,128)} async-done(((f32[64,2048]{1,0:T(8,128)}), f32[64,2048]{1,0:T(8,128)}) %all-reduce.4.cloned.1.call-update) | async-done | bytes 524304 | tf_op jit(solution)/shard_map/psum | solution.py:30
  150.6 1.3 multiply_reduce_fusion.2
  151.9 11.6 %all-reduce = (f32[64]{0:T(128)S(1)}, f32[64]{0:T(128)S(1)}, f32[64]{0:T(128)S(1)}) all-reduce(f32[64]{0:T(128)S(1)} %get-tuple-element.3, f32[64]{0:T(128)S(1)} %get-tuple-element.4, f32[64]{0:T(128)S(1)} %get-tuple-element.2), channel_id=1, replica_groups=mesh['rows'=8,'cols'=4] {'cols'}, use_global_device_ids=true, to_apply=%region_7.0 | all-reduce | flops 192 | bytes 1536 | tf_op jit(solution)/shard_map/psum | solution.py:32
  163.6 1.9 fusion.2
  165.5 0.0 reduce-scatter.5.cloned.1.call-start
  165.6 24.7 %all-gather.6.cloned.1.call-done = bf16[64,8192]{1,0:T(8,128)(2,1)} async-done(((bf16[64,2048]{1,0:T(8,128)(2,1)}), bf16[64,8192]{1,0:T(8,128)(2,1)}) %all-gather.6.cloned.1.call-update) | async-done | bytes 1048592 | tf_op jit(solution)/shard_map/all_gather | solution.py:22
  190.3 9.6 %fusion.1 = f32[64,8192]{1,0:T(8,128)} fusion(bf16[288,8192]{1,0:T(8,128)(2,1)} %param.2, bf16[64,8192]{1,0:T(8,128)(2,1)} %all-gather.6.cloned.1.call-done), kind=kOutput, calls=%fused_computation.4 | convolution fusion | flops 603998208 | bytes 7864320 | tf_op jit(solution)/shard_map/dot_general | solution.py:26
  199.9 0.0 all-reduce.6.cloned.1.call-start
  199.9 43.1 %reduce-scatter.5.cloned.1.call-done = f32[64,2048]{1,0:T(8,128)} async-done(((f32[64,8192]{1,0:T(8,128)}), f32[64,2048]{1,0:T(8,128)}) %reduce-scatter.5.cloned.1.call-update) | async-done | bytes 524304 | tf_op jit(solution)/shard_map/reduce_scatter | solution.py:29
  243.1 0.0 all-gather.8.cloned.1.call-start
  243.1 56.9 %all-reduce.6.cloned.1.call-done = f32[64,2048]{1,0:T(8,128)} async-done(((f32[64,2048]{1,0:T(8,128)}), f32[64,2048]{1,0:T(8,128)}) %all-reduce.6.cloned.1.call-update) | async-done | bytes 524304 | tf_op jit(solution)/shard_map/psum | solution.py:30
  300.1 1.4 multiply_reduce_fusion
  301.5 11.6 %psum.50 = f32[64]{0:T(128)S(1)} all-reduce(f32[64]{0:T(128)S(1)} %multiply_reduce_fusion), channel_id=1, replica_groups=mesh['rows'=8,'cols'=4] {'cols'}, use_global_device_ids=true, to_apply=%region_11.0 | all-reduce | flops 64 | bytes 512 | tf_op jit(solution)/shard_map/psum | solution.py:32
  313.1 1.1 fusion.3
  314.3 24.8 %all-gather.8.cloned.1.call-done = bf16[64,8192]{1,0:T(8,128)(2,1)} async-done(((bf16[64,2048]{1,0:T(8,128)(2,1)}), bf16[64,8192]{1,0:T(8,128)(2,1)}) %all-gather.8.cloned.1.call-update) | async-done | bytes 1048592 | tf_op jit(solution)/shard_map/all_gather | solution.py:48
  339.0 5.0 %convolution_multiply_fusion = f32[64,288]{1,0:T(8,128)} fusion(bf16[64,8192]{1,0:T(8,128)(2,1)} %all-gather.8.cloned.1.call-done, bf16[288,8192]{1,0:T(8,128)(2,1)} %param.2), kind=kOutput, calls=%fused_computation.1 | convolution fusion | flops 302008320 | bytes 5840896 | tf_op jit(solution)/shard_map/dot_general | solution.py:47
  (13 shorter events, 0.1 us)
Async XLA Ops:
  7.2 33.7 %all-gather.4.cloned.1.call-start = ((), (), s32[]{:S(2)}) async-start(), calls=%async_computation.2 | async-start | bytes 1310720 | tf_op jit(solution)/shard_map/all_gather | solution.py:22
  9.0 141.6 %copy-start = (f32[64,2048]{1,0:T(8,128)S(1)}, f32[64,2048]{1,0:T(8,128)}, u32[]{:S(2)}) copy-start(f32[64,2048]{1,0:T(8,128)} %param.3) | copy-start | bytes 1572868
  9.0 84.5 %reduce-scatter.3.cloned.1.call-start = ((), (), s32[]{:S(2)}) async-start(), calls=%async_computation.3 | async-start | bytes 2621440 | tf_op jit(solution)/shard_map/reduce_scatter | solution.py:29
  50.3 100.3 %all-reduce.4.cloned.1.call-start = ((), (), s32[]{:S(2)}) async-start(), calls=%async_computation.4 | async-start | bytes 1048576 | tf_op jit(solution)/shard_map/psum | solution.py:30
  93.5 96.8 %all-gather.6.cloned.1.call-start = ((), (), s32[]{:S(2)}) async-start(), calls=%async_computation.5 | async-start | bytes 1310720 | tf_op jit(solution)/shard_map/all_gather | solution.py:22
  165.5 134.5 %copy-start.1 = (f32[64,2048]{1,0:T(8,128)S(1)}, f32[64,2048]{1,0:T(8,128)}, u32[]{:S(2)}) copy-start(f32[64,2048]{1,0:T(8,128)} %all-reduce.4.cloned.1.call-done) | copy-start | bytes 1572868
  165.5 77.5 %reduce-scatter.5.cloned.1.call-start = ((), (), s32[]{:S(2)}) async-start(), calls=%async_computation.6 | async-start | bytes 2621440 | tf_op jit(solution)/shard_map/reduce_scatter | solution.py:29
  199.9 100.2 %all-reduce.6.cloned.1.call-start = ((), (), s32[]{:S(2)}) async-start(), calls=%async_computation.7 | async-start | bytes 1048576 | tf_op jit(solution)/shard_map/psum | solution.py:30
  243.1 95.9 %all-gather.8.cloned.1.call-start = ((), (), s32[]{:S(2)}) async-start(), calls=%async_computation.8 | async-start | bytes 1310720 | tf_op jit(solution)/shard_map/all_gather | solution.py:48
Sparse Core Ops, SparseCore 0:
  10.1 30.6 all-gather.3
  50.4 43.0 reduce-scatter.2
  96.6 53.9 all-reduce.3
  165.6 24.5 all-gather.5
  200.0 43.0 reduce-scatter.4
  246.0 53.9 all-reduce.5
  314.4 24.5 all-gather.7
where the time goes:
time: 351 us
  waiting for transfers between devices  282 us (80%)
  matrix products  24 us (7%)
  blocking collectives  23.2 us (7%)
  between operations  14.1 us (4%)
  other arithmetic  7.59 us (2%)
    psum x2, waiting for transfers between devices, per_device(): owned = lax.psum(owned, 'rows')  114 us
    reduce_scatter x2, waiting for transfers between devices, per_device(): lax.psum_scatter(partial_value, 'cols', scatter_dimension=1, tiled=True)  86.2 us
    all_gather x2, waiting for transfers between devices, per_device(): lax.all_gather(direction.astype(jnp.bfloat16), 'cols', axis=1, tiled=True)  56.5 us
    all_gather x1, waiting for transfers between devices, per_device(): lax.all_gather(solution.astype(jnp.bfloat16), 'cols', axis=1, tiled=True)  24.8 us
    psum x2, blocking collectives, per_device(): lax.psum((jnp.sum(direction * image, axis=1), jnp.sum(residual * image, a...  23.2 us
    dot_general x2, matrix products, per_device(): lax.dot_general(proj, grads, (((0,), (0,)), ((), ())), preferred_element_...  19 us
  transfers between devices with their start and end apart: 7, of which 7 were waited for; matrix products, arithmetic and copies ran while one was open for 0% of the time, Pallas kernels for 0%

commit v1 on v0

--- a/solution.py
+++ b/solution.py
@@ -2,6 +2,7 @@
 import jax.numpy as jnp
 from jax import lax
 from jax.sharding import PartitionSpec as P
+from jax.lax import axis_index, axis_size, ppermute
 
 ITERS = 2
 damping = 0.5
@@ -44,8 +45,31 @@
         if step + 1 < ITERS:
             direction = residual + (norm_next / norm_now)[:, None] * direction
             norm_now = norm_next
+
+    def _serve_group(m, across="cols"):
+        prior = axis_index(across)
+        block_last = axis_size(across)
+        m_next, far_arr, built = (block_last, prior, m.shape[1])
+        in_order = [(i0, (i0 + 1) % m_next) for i0 in range(m_next)]
+        steps_seen = [(i0, (i0 - 1) % m_next) for i0 in range(m_next)]
+        v_next = jnp.zeros((*m.shape[:1], m_next * built, *m.shape[2:]), m.dtype)
+        v_next = lax.dynamic_update_slice_in_dim(v_next, m, far_arr * built, axis=1)
+        back = m_next // 2
+        side_arr = s_next = m
+        for pp in range(1, back + 1):
+            side_arr = ppermute(side_arr, across, in_order)
+            v_next = lax.dynamic_update_slice_in_dim(
+                v_next, side_arr, (far_arr - pp) % m_next * built, axis=1
+            )
+            if pp < m_next - back:
+                s_next = ppermute(s_next, across, steps_seen)
+                v_next = lax.dynamic_update_slice_in_dim(
+                    v_next, s_next, (far_arr + pp) % m_next * built, axis=1
+                )
+        return v_next
+
     scores = lax.dot_general(
-        lax.all_gather(solution.astype(jnp.bfloat16), "cols", axis=1, tiled=True),
+        _serve_group(solution.astype(jnp.bfloat16)),
         grads,
         (((1,), (1,)), ((), ())),
         preferred_element_type=jnp.float32,

time: 351 us -> 345 us (0.983)
  waiting for transfers between devices: 282 us -> 272 us
  starting transfers between devices: 0.28 us -> 4.07 us
    all_gather x1 -> x0, waiting for transfers between devices: 24.8 us -> none  [per_device(): lax.all_gather(solution.astype(jnp.bfloat16), 'cols', axis=1, tiled=True)]
    ppermute x0 -> x3, waiting for transfers between devices: none -> 15.4 us  [the longest x2 13.6 us: _serve_group(): side_arr = ppermute(side_arr, across, in_order)]
    ppermute x0 -> x3, starting transfers between devices: none -> 3.83 us  [the longest x1 3.82 us: _serve_group(): s_next = ppermute(s_next, across, steps_seen)]
  transfers between devices with their start and end apart: 7 -> 9, of which waited for: 7 -> 9; matrix products, arithmetic and copies ran while one was open for 0% -> 0% of each run, Pallas kernels for 0% -> 0%
where the time goes in v1:
time: 345 us
  waiting for transfers between devices  272 us (79%)
  matrix products  23.6 us (7%)
  blocking collectives  23.2 us (7%)
  between operations  14.2 us (4%)
  other arithmetic  7.51 us (2%)
  starting transfers between devices  4.07 us (1%)
    psum x2, waiting for transfers between devices, per_device(): owned = lax.psum(owned, 'rows')  114 us
    reduce_scatter x2, waiting for transfers between devices, per_device(): lax.psum_scatter(partial_value, 'cols', scatter_dimension=1, tiled=True)  86.2 us
    all_gather x2, waiting for transfers between devices, per_device(): lax.all_gather(direction.astype(jnp.bfloat16), 'cols', axis=1, tiled=True)  56.5 us
    psum x2, blocking collectives, per_device(): lax.psum((jnp.sum(direction * image, axis=1), jnp.sum(residual * image, a...  23.2 us
    dot_general x2, matrix products, per_device(): lax.dot_general(proj, grads, (((0,), (0,)), ((), ())), preferred_element_...  19 us
    ppermute x2, waiting for transfers between devices, _serve_group(): side_arr = ppermute(side_arr, across, in_order)  13.6 us
  transfers between devices with their start and end apart: 9, of which 9 were waited for; matrix products, arithmetic and copies ran while one was open for 0% of the time, Pallas kernels for 0%

profile of v1, /device:TPU:0, one launch (start us, length us, event | category | flops | bytes accessed | tf_op | source)
XLA Modules:
  0.0 345.0 jit_solution(13614083318537908008)
XLA Ops:
  7.2 1.8 convert_element_type.16
  9.0 0.0 reduce-scatter.3.cloned.1.call-start
  9.1 31.8 %all-gather.3.cloned.1.call-done = bf16[64,8192]{1,0:T(8,128)(2,1)} async-done(((bf16[64,2048]{1,0:T(8,128)(2,1)}), bf16[64,8192]{1,0:T(8,128)(2,1)}) %all-gather.3.cloned.1.call-update) | async-done | bytes 1048592 | tf_op jit(solution)/shard_map/all_gather | solution.py:23
  40.9 9.4 %fusion = f32[64,8192]{1,0:T(8,128)} fusion(bf16[288,8192]{1,0:T(8,128)(2,1)} %param.2, bf16[64,8192]{1,0:T(8,128)(2,1)} %all-gather.3.cloned.1.call-done), kind=kOutput, calls=%fused_computation.2 | convolution fusion | flops 603998208 | bytes 7864320 | tf_op jit(solution)/shard_map/dot_general | solution.py:27
  50.4 43.1 %reduce-scatter.3.cloned.1.call-done = f32[64,2048]{1,0:T(8,128)} async-done(((f32[64,8192]{1,0:T(8,128)}), f32[64,2048]{1,0:T(8,128)}) %reduce-scatter.3.cloned.1.call-update) | async-done | bytes 524304 | tf_op jit(solution)/shard_map/reduce_scatter | solution.py:30
  93.5 57.1 %all-reduce.4.cloned.1.call-done = f32[64,2048]{1,0:T(8,128)} async-done(((f32[64,2048]{1,0:T(8,128)}), f32[64,2048]{1,0:T(8,128)}) %all-reduce.4.cloned.1.call-update) | async-done | bytes 524304 | tf_op jit(solution)/shard_map/psum | solution.py:31
  150.6 1.3 multiply_reduce_fusion.2
  151.9 11.6 %all-reduce = (f32[64]{0:T(128)S(1)}, f32[64]{0:T(128)S(1)}, f32[64]{0:T(128)S(1)}) all-reduce(f32[64]{0:T(128)S(1)} %get-tuple-element.3, f32[64]{0:T(128)S(1)} %get-tuple-element.4, f32[64]{0:T(128)S(1)} %get-tuple-element.2), channel_id=1, replica_groups=mesh['rows'=8,'cols'=4] {'cols'}, use_global_device_ids=true, to_apply=%region_7.0 | all-reduce | flops 192 | bytes 1536 | tf_op jit(solution)/shard_map/psum | solution.py:33
  163.6 1.9 fusion.2
  165.5 0.0 reduce-scatter.5.cloned.1.call-start
  165.6 24.7 %all-gather.5.cloned.1.call-done = bf16[64,8192]{1,0:T(8,128)(2,1)} async-done(((bf16[64,2048]{1,0:T(8,128)(2,1)}), bf16[64,8192]{1,0:T(8,128)(2,1)}) %all-gather.5.cloned.1.call-update) | async-done | bytes 1048592 | tf_op jit(solution)/shard_map/all_gather | solution.py:23
  190.3 9.6 %fusion.1 = f32[64,8192]{1,0:T(8,128)} fusion(bf16[288,8192]{1,0:T(8,128)(2,1)} %param.2, bf16[64,8192]{1,0:T(8,128)(2,1)} %all-gather.5.cloned.1.call-done), kind=kOutput, calls=%fused_computation.4 | convolution fusion | flops 603998208 | bytes 7864320 | tf_op jit(solution)/shard_map/dot_general | solution.py:27
  199.9 0.0 all-reduce.6.cloned.1.call-start
  199.9 43.1 %reduce-scatter.5.cloned.1.call-done = f32[64,2048]{1,0:T(8,128)} async-done(((f32[64,8192]{1,0:T(8,128)}), f32[64,2048]{1,0:T(8,128)}) %reduce-scatter.5.cloned.1.call-update) | async-done | bytes 524304 | tf_op jit(solution)/shard_map/reduce_scatter | solution.py:30
  243.1 57.0 %all-reduce.6.cloned.1.call-done = f32[64,2048]{1,0:T(8,128)} async-done(((f32[64,2048]{1,0:T(8,128)}), f32[64,2048]{1,0:T(8,128)}) %all-reduce.6.cloned.1.call-update) | async-done | bytes 524304 | tf_op jit(solution)/shard_map/psum | solution.py:31
  300.1 1.4 multiply_reduce_fusion
  301.5 11.6 %psum.50 = f32[64]{0:T(128)S(1)} all-reduce(f32[64]{0:T(128)S(1)} %multiply_reduce_fusion), channel_id=1, replica_groups=mesh['rows'=8,'cols'=4] {'cols'}, use_global_device_ids=true, to_apply=%region_11.0 | all-reduce | flops 64 | bytes 512 | tf_op jit(solution)/shard_map/psum | solution.py:33
  313.1 0.1 broadcast_in_dim.2
  313.2 1.1 constant_dynamic-update-slice_fusion.3
  314.2 3.8 %collective-permute-start.1 = (bf16[64,2048]{1,0:T(8,128)(2,1)S(1)}, bf16[64,2048]{1,0:T(8,128)(2,1)S(1)}, u32[]{:S(2)}, u32[]{:S(2)}) collective-permute-start(bf16[64,2048]{1,0:T(8,128)(2,1)S(1)} %get-tuple-element.9), channel_id=1, source_target_pairs={{0,3},{1,0},{2,1},{3,2},{4,7},{5,4},{6,5},{7,6},{8,11},{9,8},{10,9... | collective-permute-start | bytes 786440 | tf_op jit(solution)/shard_map/ppermute | solution.py:65
  318.1 7.3 %collective-permute-done = bf16[64,2048]{1,0:T(8,128)(2,1)S(1)} collective-permute-done((bf16[64,2048]{1,0:T(8,128)(2,1)S(1)}, bf16[64,2048]{1,0:T(8,128)(2,1)S(1)}, u32[]{:S(2)}, u32[]{:S(2)}) %collective-permute-start) | collective-permute-done | bytes 262176 | tf_op jit(solution)/shard_map/ppermute | solution.py:60
  325.3 1.8 collective-permute-done.1
  327.1 6.4 %collective-permute-done.2 = bf16[64,2048]{1,0:T(8,128)(2,1)S(1)} collective-permute-done((bf16[64,2048]{1,0:T(8,128)(2,1)S(1)}, bf16[64,2048]{1,0:T(8,128)(2,1)S(1)}, u32[]{:S(2)}, u32[]{:S(2)}) %collective-permute-start.2) | collective-permute-done | bytes 262176 | tf_op jit(solution)/shard_map/ppermute | solution.py:60
  333.5 4.6 %convolution_multiply_fusion = f32[64,288]{1,0:T(8,128)} fusion(bf16[64,8192]{1,0:T(8,128)(2,1)S(1)} %constant_dynamic-update-slice_fusion, bf16[288,8192]{1,0:T(8,128)(2,1)} %param.2), kind=kOutput, calls=%fused_computation.1 | convolution fusion | flops 302008320 | bytes 5840896 | tf_op jit(solution)/shard_map/dot_general | solution.py:71
  (20 shorter events, 0.3 us)
Async XLA Ops:
  7.2 33.7 %all-gather.3.cloned.1.call-start = ((), (), s32[]{:S(2)}) async-start(), calls=%async_computation.2 | async-start | bytes 1310720 | tf_op jit(solution)/shard_map/all_gather | solution.py:23
  9.0 141.6 %copy-start = (f32[64,2048]{1,0:T(8,128)S(1)}, f32[64,2048]{1,0:T(8,128)}, u32[]{:S(2)}) copy-start(f32[64,2048]{1,0:T(8,128)} %param.3) | copy-start | bytes 1572868
  9.0 84.5 %reduce-scatter.3.cloned.1.call-start = ((), (), s32[]{:S(2)}) async-start(), calls=%async_computation.3 | async-start | bytes 2621440 | tf_op jit(solution)/shard_map/reduce_scatter | solution.py:30
  50.3 100.3 %all-reduce.4.cloned.1.call-start = ((), (), s32[]{:S(2)}) async-start(), calls=%async_computation.4 | async-start | bytes 1048576 | tf_op jit(solution)/shard_map/psum | solution.py:31
  93.5 96.8 %all-gather.5.cloned.1.call-start = ((), (), s32[]{:S(2)}) async-start(), calls=%async_computation.5 | async-start | bytes 1310720 | tf_op jit(solution)/shard_map/all_gather | solution.py:23
  165.5 134.5 %copy-start.1 = (f32[64,2048]{1,0:T(8,128)S(1)}, f32[64,2048]{1,0:T(8,128)}, u32[]{:S(2)}) copy-start(f32[64,2048]{1,0:T(8,128)} %all-reduce.4.cloned.1.call-done) | copy-start | bytes 1572868
  165.5 77.5 %reduce-scatter.5.cloned.1.call-start = ((), (), s32[]{:S(2)}) async-start(), calls=%async_computation.6 | async-start | bytes 2621440 | tf_op jit(solution)/shard_map/reduce_scatter | solution.py:30
  199.9 100.2 %all-reduce.6.cloned.1.call-start = ((), (), s32[]{:S(2)}) async-start(), calls=%async_computation.7 | async-start | bytes 1048576 | tf_op jit(solution)/shard_map/psum | solution.py:31
  314.2 11.1 %collective-permute-start = (bf16[64,2048]{1,0:T(8,128)(2,1)S(1)}, bf16[64,2048]{1,0:T(8,128)(2,1)S(1)}, u32[]{:S(2)}, u32[]{:S(2)}) collective-permute-start(bf16[64,2048]{1,0:T(8,128)(2,1)S(1)} %get-tuple-element.9), channel_id=1, source_target_pairs={{0,1},{1,2},{2,3},{3,0},{4,5},{5,6},{6,7},{7,4},{8,9},{9,10},{10,1... | collective-permute-start | bytes 786440 | tf_op jit(solution)/shard_map/ppermute | solution.py:60
  314.2 12.9 %collective-permute-start.1 = (bf16[64,2048]{1,0:T(8,128)(2,1)S(1)}, bf16[64,2048]{1,0:T(8,128)(2,1)S(1)}, u32[]{:S(2)}, u32[]{:S(2)}) collective-permute-start(bf16[64,2048]{1,0:T(8,128)(2,1)S(1)} %get-tuple-element.9), channel_id=1, source_target_pairs={{0,3},{1,0},{2,1},{3,2},{4,7},{5,4},{6,5},{7,6},{8,11},{9,8},{10,9... | collective-permute-start | bytes 786440 | tf_op jit(solution)/shard_map/ppermute | solution.py:65
  325.3 8.2 %collective-permute-start.2 = (bf16[64,2048]{1,0:T(8,128)(2,1)S(1)}, bf16[64,2048]{1,0:T(8,128)(2,1)S(1)}, u32[]{:S(2)}, u32[]{:S(2)}) collective-permute-start(bf16[64,2048]{1,0:T(8,128)(2,1)S(1)} %collective-permute-done), channel_id=1, source_target_pairs={{0,1},{1,2},{2,3},{3,0},{4,5},{5,6},{6,7},{7,4},{8,9},{9,10},{10,1... | collective-permute-start | bytes 786440 | tf_op jit(solution)/shard_map/ppermute | solution.py:60
Sparse Core Ops, SparseCore 0:
  10.1 30.6 all-gather.2
  50.4 43.0 reduce-scatter.2
  96.6 53.9 all-reduce.3
  165.6 24.5 all-gather.4
  200.0 43.0 reduce-scatter.4
  246.0 53.9 all-reduce.5
